TPU v7x, 32 devices: a whole 2x2x4 slice. The times are simulated.
32 devices in a mesh: series: 4 (over y, x), tm: 8 (over z, core).
Axes of the slice: x: 2, y: 2, z: 4, core: 2. Of those that a mesh axis runs over, the one named last changes fastest.
Arguments:
- observed: bfloat16 [8192, 8192], P('series', 'tm'), may hold values from -6 to 6
- mask: bfloat16 [8192, 8192], P('series', 'tm'), may hold values from 0 to 1, as said below
- loadings: float32 [8192, 128], P('series'), may hold values from -0.5 to 0.5
- factors: float32 [8192, 128], P('tm'), may hold values from -6 to 6
- lag_weights: float32 [2, 128], replicated, may hold values from 0.2 to 0.7
Outputs:
- new_loadings: float32 [8192, 128], P('series')
- new_factors: float32 [8192, 128], P('tm')
Inputs may be any that keep to these rules, and one draw needn't show every extreme that they name: `mask`: each entry is 0 or 1.
All inputs are finite; a program needn't handle non-finite values.
Results may differ from a plain program's by a relative error of at most 0.0041.
Values sent between devices are 32-bit elements; how exact they have to be, the bound alone decides.
No kernel may reach another device: no remote copies, remote signals or barrier semaphores. Data moves between devices by JAX's collectives and lax.ppermute only.
A program may use at most 128 MiB of HBM per device.

v0:
```python
import jax
import jax.numpy as jnp
from jax import lax
from jax.sharding import PartitionSpec as P

LAG = 1440
OUTER = 2
TIME_STEPS = 2
smooth = 4.0
shrink = 0.1
margin = 32.0


def shifted(value, axis, steps):
    count = lax.axis_size(axis)
    initial, last = (max(0, -steps), min(count, count - steps))
    return lax.ppermute(value, axis, [(source, source + steps) for source in range(initial, last)])


def tile_residual(observed, mask, fb, xb):
    prod = lax.dot_general(fb, xb, (((1,), (1,)), ((), ())), preferred_element_type=jnp.float32)
    return (mask.astype(jnp.float32) * (prod - observed.astype(jnp.float32))).astype(jnp.bfloat16)


def smoothing(times, lag_weights):
    minutes = times.shape[0]
    whole = LAG // minutes
    rest = LAG % minutes
    before_one = jnp.concatenate(
        [shifted(times[minutes - 1 :], "tm", 1), times[: minutes - 1]], axis=0
    )
    before_far = jnp.concatenate(
        [
            shifted(times[minutes - rest :], "tm", whole + 1),
            shifted(times[: minutes - rest], "tm", whole),
        ],
        axis=0,
    )
    resid = times - lag_weights[0] * before_one - lag_weights[1] * before_far
    after_one = jnp.concatenate([resid[1:], shifted(resid[:1], "tm", -1)], axis=0)
    after_far = jnp.concatenate(
        [shifted(resid[rest:], "tm", -whole), shifted(resid[:rest], "tm", -(whole + 1))], axis=0
    )
    return smooth * (resid - lag_weights[0] * after_one - lag_weights[1] * after_far)


def body(observed, mask, loadings, factors, lag_weights):
    total_series = loadings.shape[0] * lax.axis_size("series")
    total_minutes = factors.shape[0] * lax.axis_size("tm")
    rank_width = loadings.shape[1]
    step_time = 1.0 / (total_series / rank_width + margin)
    step_load = 1.0 / total_minutes
    loads = loadings
    times = factors
    for outer in range(OUTER):
        fb = loads.astype(jnp.bfloat16)
        for inner in range(TIME_STEPS):
            xb = times.astype(jnp.bfloat16)
            rb = tile_residual(observed, mask, fb, xb)
            partial_grad = lax.dot_general(
                rb, fb, (((0,), (0,)), ((), ())), preferred_element_type=jnp.float32
            )
            smooth_grad = smoothing(times, lag_weights)
            share = lax.psum_scatter(partial_grad, "series", scatter_dimension=0, tiled=True)
            rows = share.shape[0]
            start = lax.axis_index("series") * rows
            own = lax.dynamic_slice_in_dim(times, start, rows, 0)
            own_smooth = lax.dynamic_slice_in_dim(smooth_grad, start, rows, 0)
            updated = own - step_time * (share + own_smooth)
            times = lax.all_gather(updated, "series", axis=0, tiled=True)
        xb = times.astype(jnp.bfloat16)
        rb = tile_residual(observed, mask, fb, xb)
        partial_load = jnp.dot(rb, xb, preferred_element_type=jnp.float32)
        grad_f = lax.psum(partial_load, "tm")
        loads = loads - step_load * (grad_f + shrink * loads)
    return (loads, times)


def solution(mesh):
    in_specs = (P("series", "tm"), P("series", "tm"), P("series", None), P("tm", None), P())
    out_specs = (P("series", None), P("tm", None))
    return jax.shard_map(body, mesh=mesh, in_specs=in_specs, out_specs=out_specs, check_vma=False)
```

profile of v0, /device:TPU:0, one launch (start us, length us, event | category | flops | bytes accessed | tf_op | source)
XLA Modules:
  0.0 333.9 jit_solution(2569922140256793986)
XLA Ops:
  7.2 9.1 %fusion.11 = f32[1024,128]{1,0:T(8,128)} fusion(bf16[2048,1024]{1,0:T(8,128)(2,1)} %param.6, bf16[2048,1024]{1,0:T(8,128)(2,1)} %param.5, f32[1024,128]{1,0:T(8,128)} %param.8, f32[2048,128]{1,0:T(8,128)} %param.7), kind=kOutput, calls=%fused_computation.23 | convolution fusion | flops 1084882944 | bytes 10485760 | tf_op jit(solution)/shard_map/dot_general | solution.py:60
  16.4 2.5 collective-permute-start.2
  19.0 4.6 %collective-permute-start = (f32[1,128]{1,0:T(1,128)S(1)}, f32[1,128]{1,0:T(1,128)S(1)}, u32[]{:S(2)}, u32[]{:S(2)}) collective-permute-start(f32[1,128]{1,0:T(1,128)S(1)} %slice.117), channel_id=1, source_target_pairs={{0,1},{1,2},{2,3},{3,4},{4,5},{5,6},{6,7},{8,9},{9,10},{10,11},{11... | collective-permute-start | bytes 1544 | tf_op jit(solution)/shard_map/ppermute | solution.py:17
  23.6 3.5 %collective-permute-start.1 = (f32[416,128]{1,0:T(8,128)S(1)}, f32[416,128]{1,0:T(8,128)S(1)}, u32[]{:S(2)}, u32[]{:S(2)}) collective-permute-start(f32[416,128]{1,0:T(8,128)S(1)} %slice.120), channel_id=1, source_target_pairs={{0,2},{1,3},{2,4},{3,5},{4,6},{5,7},{8,10},{9,11},{10,12},{11,13},... | collective-permute-start | bytes 638984 | tf_op jit(solution)/shard_map/ppermute | solution.py:17
  27.1 4.6 %collective-permute-done.1 = f32[416,128]{1,0:T(8,128)S(1)} collective-permute-done((f32[416,128]{1,0:T(8,128)S(1)}, f32[416,128]{1,0:T(8,128)S(1)}, u32[]{:S(2)}, u32[]{:S(2)}) %collective-permute-start.1) | collective-permute-done | bytes 213024 | tf_op jit(solution)/shard_map/ppermute | solution.py:17
  36.5 2.3 collective-permute-done.3
  38.9 6.8 %collective-permute-done.5 = f32[416,128]{1,0:T(8,128)S(1)} collective-permute-done((f32[416,128]{1,0:T(8,128)}, f32[416,128]{1,0:T(8,128)S(1)}, u32[]{:S(2)}, u32[]{:S(2)}) %collective-permute-start.5) | collective-permute-done | bytes 213024 | tf_op jit(solution)/shard_map/ppermute | solution.py:17
  46.8 10.0 %all_gather.12 = f32[1024,128]{1,0:T(8,128)S(1)} all-gather(f32[256,128]{1,0:T(8,128)S(1)} %fusion.65), channel_id=1, replica_groups=mesh['series'=4,'tm'=8] {'series'}, dimensions={0}, use_global_device_ids=true | all-gather | bytes 655360 | tf_op jit(solution)/shard_map/all_gather | solution.py:70
  56.8 8.2 %fusion.10 = f32[1024,128]{1,0:T(8,128)} fusion(bf16[2048,1024]{1,0:T(8,128)(2,1)} %param.6, bf16[2048,1024]{1,0:T(8,128)(2,1)} %param.5, f32[1024,128]{1,0:T(8,128)S(1)} %all_gather.12, f32[2048,128]{1,0:T(8,128)S(1)} %copy-done), kind=kOutput, calls=%fused_computation.22 | convolution fusion | flops 1084882944 | bytes 10485760 | tf_op jit(solution)/shard_map/dot_general | solution.py:60
  66.5 4.1 %collective-permute-start.7 = (f32[416,128]{1,0:T(8,128)S(1)}, f32[416,128]{1,0:T(8,128)S(1)}, u32[]{:S(2)}, u32[]{:S(2)}) collective-permute-start(f32[416,128]{1,0:T(8,128)S(1)} %slice.156), channel_id=1, source_target_pairs={{0,2},{1,3},{2,4},{3,5},{4,6},{5,7},{8,10},{9,11},{10,12},{11,13},... | collective-permute-start | bytes 638984 | tf_op jit(solution)/shard_map/ppermute | solution.py:17
  70.6 2.8 collective-permute-start.6
  74.2 2.0 collective-permute-done.7
  80.4 2.8 collective-permute-done.9
  83.2 7.9 %collective-permute-done.11 = f32[416,128]{1,0:T(8,128)S(1)} collective-permute-done((f32[416,128]{1,0:T(8,128)S(1)}, f32[416,128]{1,0:T(8,128)S(1)}, u32[]{:S(2)}, u32[]{:S(2)}) %collective-permute-start.11) | collective-permute-done | bytes 213024 | tf_op jit(solution)/shard_map/ppermute | solution.py:17
  92.1 10.0 %all_gather.13 = f32[1024,128]{1,0:T(8,128)S(1)} all-gather(f32[256,128]{1,0:T(8,128)S(1)} %fusion.55), channel_id=1, replica_groups=mesh['series'=4,'tm'=8] {'series'}, dimensions={0}, use_global_device_ids=true | all-gather | bytes 655360 | tf_op jit(solution)/shard_map/all_gather | solution.py:70
  102.1 6.9 %fusion.7 = f32[2048,128]{1,0:T(8,128)} fusion(bf16[2048,1024]{1,0:T(8,128)(2,1)} %param.6, bf16[2048,1024]{1,0:T(8,128)(2,1)} %param.5, f32[1024,128]{1,0:T(8,128)S(1)} %all_gather.13, f32[2048,128]{1,0:T(8,128)S(1)} %copy-done), kind=kOutput, calls=%fused_computation.19 | convolution fusion | flops 1084751872 | bytes 11010048 | tf_op jit(solution)/shard_map/dot_general | solution.py:73
  109.2 57.6 %all-reduce.3.cloned.1.call-done = f32[2048,128]{1,0:T(8,128)} async-done(((f32[2048,128]{1,0:T(8,128)}), f32[2048,128]{1,0:T(8,128)}) %all-reduce.3.cloned.1.call-update) | async-done | bytes 1048592 | tf_op jit(solution)/shard_map/psum | solution.py:74
  168.3 8.2 %fusion.9 = f32[1024,128]{1,0:T(8,128)} fusion(bf16[2048,128]{1,0:T(8,128)(2,1)S(1)} %fusion.20, bf16[2048,1024]{1,0:T(8,128)(2,1)} %param.6, bf16[2048,1024]{1,0:T(8,128)(2,1)} %param.5, f32[1024,128]{1,0:T(8,128)S(1)} %all_gather.13), kind=kOutput, calls=%fused_computation.21 | convolution fusion | flops 1084358656 | bytes 9961472 | tf_op jit(solution)/shard_map/dot_general | solution.py:60
  178.0 3.2 collective-permute-start.13
  181.2 3.1 collective-permute-start.12
  190.9 2.8 collective-permute-done.15
  193.7 8.0 %collective-permute-done.17 = f32[416,128]{1,0:T(8,128)} collective-permute-done((f32[416,128]{1,0:T(8,128)S(1)}, f32[416,128]{1,0:T(8,128)}, u32[]{:S(2)}, u32[]{:S(2)}) %collective-permute-start.17) | collective-permute-done | bytes 213024 | tf_op jit(solution)/shard_map/ppermute | solution.py:17
  202.7 10.0 %all_gather.14 = f32[1024,128]{1,0:T(8,128)S(1)} all-gather(f32[256,128]{1,0:T(8,128)S(1)} %fusion.45), channel_id=1, replica_groups=mesh['series'=4,'tm'=8] {'series'}, dimensions={0}, use_global_device_ids=true | all-gather | bytes 655360 | tf_op jit(solution)/shard_map/all_gather | solution.py:70
  212.8 8.2 %fusion.8 = f32[1024,128]{1,0:T(8,128)} fusion(bf16[2048,128]{1,0:T(8,128)(2,1)S(1)} %fusion.20, bf16[2048,1024]{1,0:T(8,128)(2,1)} %param.6, bf16[2048,1024]{1,0:T(8,128)(2,1)} %param.5, f32[1024,128]{1,0:T(8,128)S(1)} %all_gather.14), kind=kOutput, calls=%fused_computation.20 | convolution fusion | flops 1084358656 | bytes 9961472 | tf_op jit(solution)/shard_map/dot_general | solution.py:60
  222.5 4.3 %collective-permute-start.19 = (f32[416,128]{1,0:T(8,128)S(1)}, f32[416,128]{1,0:T(8,128)S(1)}, u32[]{:S(2)}, u32[]{:S(2)}) collective-permute-start(f32[416,128]{1,0:T(8,128)S(1)} %slice.172), channel_id=1, source_target_pairs={{0,2},{1,3},{2,4},{3,5},{4,6},{5,7},{8,10},{9,11},{10,12},{11,13},... | collective-permute-start | bytes 638984 | tf_op jit(solution)/shard_map/ppermute | solution.py:17
  226.8 3.1 collective-permute-start.18
  236.5 2.8 collective-permute-done.21
  239.3 8.0 %collective-permute-done.23 = f32[416,128]{1,0:T(8,128)} collective-permute-done((f32[416,128]{1,0:T(8,128)S(1)}, f32[416,128]{1,0:T(8,128)}, u32[]{:S(2)}, u32[]{:S(2)}) %collective-permute-start.23) | collective-permute-done | bytes 213024 | tf_op jit(solution)/shard_map/ppermute | solution.py:17
  248.3 10.1 %all_gather.15 = f32[1024,128]{1,0:T(8,128)S(1)} all-gather(f32[256,128]{1,0:T(8,128)S(1)} %fusion.35), channel_id=1, replica_groups=mesh['series'=4,'tm'=8] {'series'}, dimensions={0}, use_global_device_ids=true | all-gather | bytes 655360 | tf_op jit(solution)/shard_map/all_gather | solution.py:70
  258.4 7.0 %fusion.6 = f32[2048,128]{1,0:T(8,128)} fusion(bf16[2048,1024]{1,0:T(8,128)(2,1)} %param.6, bf16[2048,1024]{1,0:T(8,128)(2,1)} %param.5, bf16[2048,128]{1,0:T(8,128)(2,1)S(1)} %fusion.20, f32[1024,128]{1,0:T(8,128)S(1)} %all_gather.15), kind=kOutput, calls=%fused_computation.18 | convolution fusion | flops 1084489728 | bytes 10485760 | tf_op jit(solution)/shard_map/dot_general | solution.py:73
  265.4 58.4 %all-reduce.5.cloned.1.call-done = f32[2048,128]{1,0:T(8,128)} async-done(((f32[2048,128]{1,0:T(8,128)}), f32[2048,128]{1,0:T(8,128)}) %all-reduce.5.cloned.1.call-update) | async-done | bytes 1048592 | tf_op jit(solution)/shard_map/psum | solution.py:74
  323.8 2.5 multiply_subtract_fusion
  (92 shorter events, 33.8 us)
Async XLA Ops:
  7.2 38.5 %reduce-scatter.5.cloned.1.call-start = ((), (), s32[]{:S(2)}) async-start(), calls=%async_computation.4 | async-start | bytes 655360 | tf_op jit(solution)/shard_map/reduce_scatter | solution.py:64
  16.3 40.5 %copy-start = (f32[2048,128]{1,0:T(8,128)S(1)}, f32[2048,128]{1,0:T(8,128)}, u32[]{:S(2)}) copy-start(f32[2048,128]{1,0:T(8,128)} %param.7) | copy-start | bytes 3145732
  16.3 74.7 %reduce-scatter.7.cloned.1.call-start = ((), (), s32[]{:S(2)}) async-start(), calls=%async_computation.5 | async-start | bytes 655360 | tf_op jit(solution)/shard_map/reduce_scatter | solution.py:64
  16.4 15.3 %collective-permute-start.2 = (f32[608,128]{1,0:T(8,128)S(1)}, f32[608,128]{1,0:T(8,128)S(1)}, u32[]{:S(2)}, u32[]{:S(2)}) collective-permute-start(f32[608,128]{1,0:T(8,128)S(1)} %slice.121), channel_id=1, source_target_pairs={{0,1},{1,2},{2,3},{3,4},{4,5},{5,6},{6,7},{8,9},{9,10},{10,11},{11... | collective-permute-start | bytes 933896 | tf_op jit(solution)/shard_map/ppermute | solution.py:17
  19.0 8.1 %collective-permute-start = (f32[1,128]{1,0:T(1,128)S(1)}, f32[1,128]{1,0:T(1,128)S(1)}, u32[]{:S(2)}, u32[]{:S(2)}) collective-permute-start(f32[1,128]{1,0:T(1,128)S(1)} %slice.117), channel_id=1, source_target_pairs={{0,1},{1,2},{2,3},{3,4},{4,5},{5,6},{6,7},{8,9},{9,10},{10,11},{11... | collective-permute-start | bytes 1544 | tf_op jit(solution)/shard_map/ppermute | solution.py:17
  23.6 8.2 %collective-permute-start.1 = (f32[416,128]{1,0:T(8,128)S(1)}, f32[416,128]{1,0:T(8,128)S(1)}, u32[]{:S(2)}, u32[]{:S(2)}) collective-permute-start(f32[416,128]{1,0:T(8,128)S(1)} %slice.120), channel_id=1, source_target_pairs={{0,2},{1,3},{2,4},{3,5},{4,6},{5,7},{8,10},{9,11},{10,12},{11,13},... | collective-permute-start | bytes 638984 | tf_op jit(solution)/shard_map/ppermute | solution.py:17
  31.9 13.8 %collective-permute-start.4 = (f32[608,128]{1,0:T(8,128)S(1)}, f32[608,128]{1,0:T(8,128)S(1)}, u32[]{:S(2)}, u32[]{:S(2)}) collective-permute-start(f32[608,128]{1,0:T(8,128)S(1)} %slice.152), channel_id=1, source_target_pairs={{1,0},{2,1},{3,2},{4,3},{5,4},{6,5},{7,6},{9,8},{10,9},{11,10},{12... | collective-permute-start | bytes 933896 | tf_op jit(solution)/shard_map/ppermute | solution.py:17
  33.9 11.8 %collective-permute-start.5 = (f32[416,128]{1,0:T(8,128)}, f32[416,128]{1,0:T(8,128)S(1)}, u32[]{:S(2)}, u32[]{:S(2)}) collective-permute-start(f32[416,128]{1,0:T(8,128)} %slice.153), channel_id=1, source_target_pairs={{2,0},{3,1},{4,2},{5,3},{6,4},{7,5},{10,8},{11,9},{12,10},{13,11},... | collective-permute-start | bytes 638984 | tf_op jit(solution)/shard_map/ppermute | solution.py:17
  35.2 3.7 %collective-permute-start.3 = (f32[1,128]{1,0:T(1,128)S(1)}, f32[1,128]{1,0:T(1,128)S(1)}, u32[]{:S(2)}, u32[]{:S(2)}) collective-permute-start(f32[1,128]{1,0:T(1,128)S(1)} %slice.151), channel_id=1, source_target_pairs={{1,0},{2,1},{3,2},{4,3},{5,4},{6,5},{7,6},{9,8},{10,9},{11,10},{12... | collective-permute-start | bytes 1544 | tf_op jit(solution)/shard_map/ppermute | solution.py:17
  65.1 101.8 %all-reduce.3.cloned.1.call-start = ((), (), s32[]{:S(2)}) async-start(), calls=%async_computation.6 | async-start | bytes 2097152 | tf_op jit(solution)/shard_map/psum | solution.py:74
  65.2 11.1 %collective-permute-start.8 = (f32[608,128]{1,0:T(8,128)S(1)}, f32[608,128]{1,0:T(8,128)S(1)}, u32[]{:S(2)}, u32[]{:S(2)}) collective-permute-start(f32[608,128]{1,0:T(8,128)S(1)} %slice.157), channel_id=1, source_target_pairs={{0,1},{1,2},{2,3},{3,4},{4,5},{5,6},{6,7},{8,9},{9,10},{10,11},{11... | collective-permute-start | bytes 933896 | tf_op jit(solution)/shard_map/ppermute | solution.py:17
  66.5 9.7 %collective-permute-start.7 = (f32[416,128]{1,0:T(8,128)S(1)}, f32[416,128]{1,0:T(8,128)S(1)}, u32[]{:S(2)}, u32[]{:S(2)}) collective-permute-start(f32[416,128]{1,0:T(8,128)S(1)} %slice.156), channel_id=1, source_target_pairs={{0,2},{1,3},{2,4},{3,5},{4,6},{5,7},{8,10},{9,11},{10,12},{11,13},... | collective-permute-start | bytes 638984 | tf_op jit(solution)/shard_map/ppermute | solution.py:17
  70.6 3.6 %collective-permute-start.6 = (f32[1,128]{1,0:T(1,128)S(1)}, f32[1,128]{1,0:T(1,128)S(1)}, u32[]{:S(2)}, u32[]{:S(2)}) collective-permute-start(f32[1,128]{1,0:T(1,128)S(1)} %slice.154), channel_id=1, source_target_pairs={{0,1},{1,2},{2,3},{3,4},{4,5},{5,6},{6,7},{8,9},{9,10},{10,11},{11... | collective-permute-start | bytes 1544 | tf_op jit(solution)/shard_map/ppermute | solution.py:17
  76.4 14.6 %collective-permute-start.10 = (f32[608,128]{1,0:T(8,128)S(1)}, f32[608,128]{1,0:T(8,128)S(1)}, u32[]{:S(2)}, u32[]{:S(2)}) collective-permute-start(f32[608,128]{1,0:T(8,128)S(1)} %slice.160), channel_id=1, source_target_pairs={{1,0},{2,1},{3,2},{4,3},{5,4},{6,5},{7,6},{9,8},{10,9},{11,10},{12... | collective-permute-start | bytes 933896 | tf_op jit(solution)/shard_map/ppermute | solution.py:17
  77.7 13.3 %collective-permute-start.11 = (f32[416,128]{1,0:T(8,128)S(1)}, f32[416,128]{1,0:T(8,128)S(1)}, u32[]{:S(2)}, u32[]{:S(2)}) collective-permute-start(f32[416,128]{1,0:T(8,128)S(1)} %slice.161), channel_id=1, source_target_pairs={{2,0},{3,1},{4,2},{5,3},{6,4},{7,5},{10,8},{11,9},{12,10},{13,11},... | collective-permute-start | bytes 638984 | tf_op jit(solution)/shard_map/ppermute | solution.py:17
  79.0 4.2 %collective-permute-start.9 = (f32[1,128]{1,0:T(1,128)S(1)}, f32[1,128]{1,0:T(1,128)S(1)}, u32[]{:S(2)}, u32[]{:S(2)}) collective-permute-start(f32[1,128]{1,0:T(1,128)S(1)} %slice.159), channel_id=1, source_target_pairs={{1,0},{2,1},{3,2},{4,3},{5,4},{6,5},{7,6},{9,8},{10,9},{11,10},{12... | collective-permute-start | bytes 1544 | tf_op jit(solution)/shard_map/ppermute | solution.py:17
  109.0 92.7 %reduce-scatter.9.cloned.1.call-start = ((), (), s32[]{:S(2)}) async-start(), calls=%async_computation.7 | async-start | bytes 655360 | tf_op jit(solution)/shard_map/reduce_scatter | solution.py:64
  176.6 70.7 %reduce-scatter.11.cloned.1.call-start = ((), (), s32[]{:S(2)}) async-start(), calls=%async_computation.8 | async-start | bytes 655360 | tf_op jit(solution)/shard_map/reduce_scatter | solution.py:64
  176.6 10.1 %collective-permute-start.14 = (f32[608,128]{1,0:T(8,128)S(1)}, f32[608,128]{1,0:T(8,128)S(1)}, u32[]{:S(2)}, u32[]{:S(2)}) collective-permute-start(f32[608,128]{1,0:T(8,128)S(1)} %slice.165), channel_id=1, source_target_pairs={{0,1},{1,2},{2,3},{3,4},{4,5},{5,6},{6,7},{8,9},{9,10},{10,11},{11... | collective-permute-start | bytes 933896 | tf_op jit(solution)/shard_map/ppermute | solution.py:17
  178.0 8.8 %collective-permute-start.13 = (f32[416,128]{1,0:T(8,128)S(1)}, f32[416,128]{1,0:T(8,128)S(1)}, u32[]{:S(2)}, u32[]{:S(2)}) collective-permute-start(f32[416,128]{1,0:T(8,128)S(1)} %slice.164), channel_id=1, source_target_pairs={{0,2},{1,3},{2,4},{3,5},{4,6},{5,7},{8,10},{9,11},{10,12},{11,13},... | collective-permute-start | bytes 638984 | tf_op jit(solution)/shard_map/ppermute | solution.py:17
  181.2 3.9 %collective-permute-start.12 = (f32[1,128]{1,0:T(1,128)S(1)}, f32[1,128]{1,0:T(1,128)S(1)}, u32[]{:S(2)}, u32[]{:S(2)}) collective-permute-start(f32[1,128]{1,0:T(1,128)S(1)} %slice.162), channel_id=1, source_target_pairs={{0,1},{1,2},{2,3},{3,4},{4,5},{5,6},{6,7},{8,9},{9,10},{10,11},{11... | collective-permute-start | bytes 1544 | tf_op jit(solution)/shard_map/ppermute | solution.py:17
  186.9 14.8 %collective-permute-start.16 = (f32[608,128]{1,0:T(8,128)S(1)}, f32[608,128]{1,0:T(8,128)S(1)}, u32[]{:S(2)}, u32[]{:S(2)}) collective-permute-start(f32[608,128]{1,0:T(8,128)S(1)} %slice.168), channel_id=1, source_target_pairs={{1,0},{2,1},{3,2},{4,3},{5,4},{6,5},{7,6},{9,8},{10,9},{11,10},{12... | collective-permute-start | bytes 933896 | tf_op jit(solution)/shard_map/ppermute | solution.py:17
  188.2 13.4 %collective-permute-start.17 = (f32[416,128]{1,0:T(8,128)S(1)}, f32[416,128]{1,0:T(8,128)}, u32[]{:S(2)}, u32[]{:S(2)}) collective-permute-start(f32[416,128]{1,0:T(8,128)S(1)} %slice.169), channel_id=1, source_target_pairs={{2,0},{3,1},{4,2},{5,3},{6,4},{7,5},{10,8},{11,9},{12,10},{13,11},... | collective-permute-start | bytes 638984 | tf_op jit(solution)/shard_map/ppermute | solution.py:17
  189.6 4.2 %collective-permute-start.15 = (f32[1,128]{1,0:T(1,128)S(1)}, f32[1,128]{1,0:T(1,128)S(1)}, u32[]{:S(2)}, u32[]{:S(2)}) collective-permute-start(f32[1,128]{1,0:T(1,128)S(1)} %slice.167), channel_id=1, source_target_pairs={{1,0},{2,1},{3,2},{4,3},{5,4},{6,5},{7,6},{9,8},{10,9},{11,10},{12... | collective-permute-start | bytes 1544 | tf_op jit(solution)/shard_map/ppermute | solution.py:17
  221.0 102.7 %all-reduce.5.cloned.1.call-start = ((), (), s32[]{:S(2)}) async-start(), calls=%async_computation.9 | async-start | bytes 2097152 | tf_op jit(solution)/shard_map/psum | solution.py:74
  221.1 11.3 %collective-permute-start.20 = (f32[608,128]{1,0:T(8,128)S(1)}, f32[608,128]{1,0:T(8,128)S(1)}, u32[]{:S(2)}, u32[]{:S(2)}) collective-permute-start(f32[608,128]{1,0:T(8,128)S(1)} %slice.173), channel_id=1, source_target_pairs={{0,1},{1,2},{2,3},{3,4},{4,5},{5,6},{6,7},{8,9},{9,10},{10,11},{11... | collective-permute-start | bytes 933896 | tf_op jit(solution)/shard_map/ppermute | solution.py:17
  222.5 9.9 %collective-permute-start.19 = (f32[416,128]{1,0:T(8,128)S(1)}, f32[416,128]{1,0:T(8,128)S(1)}, u32[]{:S(2)}, u32[]{:S(2)}) collective-permute-start(f32[416,128]{1,0:T(8,128)S(1)} %slice.172), channel_id=1, source_target_pairs={{0,2},{1,3},{2,4},{3,5},{4,6},{5,7},{8,10},{9,11},{10,12},{11,13},... | collective-permute-start | bytes 638984 | tf_op jit(solution)/shard_map/ppermute | solution.py:17
  226.8 3.9 %collective-permute-start.18 = (f32[1,128]{1,0:T(1,128)S(1)}, f32[1,128]{1,0:T(1,128)S(1)}, u32[]{:S(2)}, u32[]{:S(2)}) collective-permute-start(f32[1,128]{1,0:T(1,128)S(1)} %slice.170), channel_id=1, source_target_pairs={{0,1},{1,2},{2,3},{3,4},{4,5},{5,6},{6,7},{8,9},{9,10},{10,11},{11... | collective-permute-start | bytes 1544 | tf_op jit(solution)/shard_map/ppermute | solution.py:17
  232.5 14.8 %collective-permute-start.22 = (f32[608,128]{1,0:T(8,128)S(1)}, f32[608,128]{1,0:T(8,128)S(1)}, u32[]{:S(2)}, u32[]{:S(2)}) collective-permute-start(f32[608,128]{1,0:T(8,128)S(1)} %slice.176), channel_id=1, source_target_pairs={{1,0},{2,1},{3,2},{4,3},{5,4},{6,5},{7,6},{9,8},{10,9},{11,10},{12... | collective-permute-start | bytes 933896 | tf_op jit(solution)/shard_map/ppermute | solution.py:17
  233.9 13.4 %collective-permute-start.23 = (f32[416,128]{1,0:T(8,128)S(1)}, f32[416,128]{1,0:T(8,128)}, u32[]{:S(2)}, u32[]{:S(2)}) collective-permute-start(f32[416,128]{1,0:T(8,128)S(1)} %slice.177), channel_id=1, source_target_pairs={{2,0},{3,1},{4,2},{5,3},{6,4},{7,5},{10,8},{11,9},{12,10},{13,11},... | collective-permute-start | bytes 638984 | tf_op jit(solution)/shard_map/ppermute | solution.py:17
  235.2 4.2 %collective-permute-start.21 = (f32[1,128]{1,0:T(1,128)S(1)}, f32[1,128]{1,0:T(1,128)S(1)}, u32[]{:S(2)}, u32[]{:S(2)}) collective-permute-start(f32[1,128]{1,0:T(1,128)S(1)} %slice.175), channel_id=1, source_target_pairs={{1,0},{2,1},{3,2},{4,3},{5,4},{6,5},{7,6},{9,8},{10,9},{11,10},{12... | collective-permute-start | bytes 1544 | tf_op jit(solution)/shard_map/ppermute | solution.py:17
  258.4 65.4 %copy-start.2 = (f32[2048,128]{1,0:T(8,128)S(1)}, f32[2048,128]{1,0:T(8,128)}, u32[]{:S(2)}) copy-start(f32[2048,128]{1,0:T(8,128)} %all-reduce.3.cloned.1.call-done) | copy-start | bytes 3145732
  (2 other events, 29.1 us)
Sparse Core Ops, SparseCore 0:
  16.4 27.8 reduce-scatter.4
  65.2 23.8 reduce-scatter.6
  109.1 57.7 all-reduce.2
  176.7 24.1 reduce-scatter.8
  221.2 24.5 reduce-scatter.10
  265.5 58.2 all-reduce.4
where the time goes:
time: 335 us; the launch traced here: 334 us
  waiting for transfers between devices  170 us (51%)
  starting transfers between devices  51 us (15%)
  matrix products  47.7 us (14%)
  blocking collectives  40.2 us (12%)
  between operations  14.6 us (4%)
  other arithmetic  8.5 us (3%)
    psum x2, waiting for transfers between devices, body(): grad_f = lax.psum(partial_load, 'tm')  116 us
    ppermute x24, waiting for transfers between devices, shifted(): lax.ppermute(value, axis, [(source, source + steps) for source in range(i...  53.9 us
    ppermute x24, starting transfers between devices, shifted(): lax.ppermute(value, axis, [(source, source + steps) for source in range(i...  50.6 us
    all_gather x4, blocking collectives, body(): times = lax.all_gather(updated, 'series', axis=0, tiled=True)  40.2 us
    dot_general x4, matrix products, body(): lax.dot_general(rb, fb, (((0,), (0,)), ((), ())), preferred_element_type=...  33.8 us
    dot_general x2, matrix products, body(): partial_load = jnp.dot(rb, xb, preferred_element_type=jnp.float32)  13.9 us
  transfers between devices with their start and end apart: 30, of which 17 were waited for; matrix products, arithmetic and copies ran while one was open for 0% of the time, Pallas kernels for 0%

commit v1 on v0

--- a/solution.py
+++ b/solution.py
@@ -71,7 +71,9 @@
         xb = times.astype(jnp.bfloat16)
         rb = tile_residual(observed, mask, fb, xb)
         partial_load = jnp.dot(rb, xb, preferred_element_type=jnp.float32)
-        grad_f = lax.psum(partial_load, "tm")
+        grad_f = partial_load
+        for hop in (1, 2, 4):
+            grad_f = grad_f + lax.ppermute(grad_f, "tm", [(dev, dev ^ hop) for dev in range(8)])
         loads = loads - step_load * (grad_f + shrink * loads)
     return (loads, times)
 

time: 335 us -> 364 us (1.087)
  waiting for transfers between devices: 170 us -> 197 us
  starting transfers between devices: 51 us -> 57.1 us
    ppermute x0 -> x6, waiting for transfers between devices: none -> 144 us  [body(): lax.ppermute(grad_f, 'tm', [(dev, dev ^ hop) for dev in range(8)])]
    psum x2 -> x0, waiting for transfers between devices: 116 us -> none  [body(): grad_f = lax.psum(partial_load, 'tm')]
    ppermute x0 -> x6, starting transfers between devices: none -> 7.95 us  [body(): lax.ppermute(grad_f, 'tm', [(dev, dev ^ hop) for dev in range(8)])]
  transfers between devices with their start and end apart: 30 -> 34, of which waited for: 17 -> 22; matrix products, arithmetic and copies ran while one was open for 0% -> 0% of each run, Pallas kernels for 0% -> 0%
where the time goes in v1:
time: 364 us; the launch traced here: 363 us
  waiting for transfers between devices  197 us (54%)
  starting transfers between devices  57.1 us (16%)
  matrix products  45.5 us (12%)
  blocking collectives  39.9 us (11%)
  between operations  14.3 us (4%)
  other arithmetic  6.56 us (2%)
    ppermute x6, waiting for transfers between devices, body(): lax.ppermute(grad_f, 'tm', [(dev, dev ^ hop) for dev in range(8)])  144 us
    ppermute x24, waiting for transfers between devices, shifted(): lax.ppermute(value, axis, [(source, source + steps) for source in range(i...  53.3 us
    ppermute x24, starting transfers between devices, shifted(): lax.ppermute(value, axis, [(source, source + steps) for source in range(i...  49 us
    all_gather x4, blocking collectives, body(): times = lax.all_gather(updated, 'series', axis=0, tiled=True)  39.9 us
    dot_general x4, matrix products, body(): lax.dot_general(rb, fb, (((0,), (0,)), ((), ())), preferred_element_type=...  33.7 us
    dot_general x2, matrix products, body(): partial_load = jnp.dot(rb, xb, preferred_element_type=jnp.float32)  11.8 us
    ppermute x6, starting transfers between devices, body(): lax.ppermute(grad_f, 'tm', [(dev, dev ^ hop) for dev in range(8)])  7.95 us
  transfers between devices with their start and end apart: 34, of which 22 were waited for; matrix products, arithmetic and copies ran while one was open for 0% of the time, Pallas kernels for 0%

profile of v1, /device:TPU:0, one launch (start us, length us, event | category | flops | bytes accessed | tf_op | source)
XLA Modules:
  0.0 362.6 jit_solution(10533224339401197446)
XLA Ops:
  7.2 9.0 %fusion.11 = f32[1024,128]{1,0:T(8,128)} fusion(bf16[2048,1024]{1,0:T(8,128)(2,1)} %param.6, bf16[2048,1024]{1,0:T(8,128)(2,1)} %param.5, f32[1024,128]{1,0:T(8,128)} %param.8, f32[2048,128]{1,0:T(8,128)} %param.7), kind=kOutput, calls=%fused_computation.23 | convolution fusion | flops 1084882944 | bytes 10485760 | tf_op jit(solution)/shard_map/dot_general | solution.py:60
  18.9 4.6 %collective-permute-start = (f32[1,128]{1,0:T(1,128)S(1)}, f32[1,128]{1,0:T(1,128)S(1)}, u32[]{:S(2)}, u32[]{:S(2)}) collective-permute-start(f32[1,128]{1,0:T(1,128)S(1)} %slice.117), channel_id=1, source_target_pairs={{0,1},{1,2},{2,3},{3,4},{4,5},{5,6},{6,7},{8,9},{9,10},{10,11},{11... | collective-permute-start | bytes 1544 | tf_op jit(solution)/shard_map/ppermute | solution.py:17
  23.5 3.5 collective-permute-start.1
  27.0 4.6 %collective-permute-done.1 = f32[416,128]{1,0:T(8,128)S(1)} collective-permute-done((f32[416,128]{1,0:T(8,128)S(1)}, f32[416,128]{1,0:T(8,128)S(1)}, u32[]{:S(2)}, u32[]{:S(2)}) %collective-permute-start.1) | collective-permute-done | bytes 213024 | tf_op jit(solution)/shard_map/ppermute | solution.py:17
  38.8 6.8 %collective-permute-done.5 = f32[416,128]{1,0:T(8,128)S(1)} collective-permute-done((f32[416,128]{1,0:T(8,128)}, f32[416,128]{1,0:T(8,128)S(1)}, u32[]{:S(2)}, u32[]{:S(2)}) %collective-permute-start.5) | collective-permute-done | bytes 213024 | tf_op jit(solution)/shard_map/ppermute | solution.py:17
  46.7 10.0 %all_gather.12 = f32[1024,128]{1,0:T(8,128)S(1)} all-gather(f32[256,128]{1,0:T(8,128)S(1)} %fusion.64), channel_id=1, replica_groups=mesh['series'=4,'tm'=8] {'series'}, dimensions={0}, use_global_device_ids=true | all-gather | bytes 655360 | tf_op jit(solution)/shard_map/all_gather | solution.py:70
  56.7 8.2 %fusion.10 = f32[1024,128]{1,0:T(8,128)} fusion(bf16[2048,1024]{1,0:T(8,128)(2,1)} %param.6, bf16[2048,1024]{1,0:T(8,128)(2,1)} %param.5, f32[1024,128]{1,0:T(8,128)S(1)} %all_gather.12, f32[2048,128]{1,0:T(8,128)S(1)} %copy-done), kind=kOutput, calls=%fused_computation.22 | convolution fusion | flops 1084882944 | bytes 10485760 | tf_op jit(solution)/shard_map/dot_general | solution.py:60
  66.4 4.1 %collective-permute-start.7 = (f32[416,128]{1,0:T(8,128)S(1)}, f32[416,128]{1,0:T(8,128)S(1)}, u32[]{:S(2)}, u32[]{:S(2)}) collective-permute-start(f32[416,128]{1,0:T(8,128)S(1)} %slice.156), channel_id=1, source_target_pairs={{0,2},{1,3},{2,4},{3,5},{4,6},{5,7},{8,10},{9,11},{10,12},{11,13},... | collective-permute-start | bytes 638984 | tf_op jit(solution)/shard_map/ppermute | solution.py:17
  70.5 2.8 collective-permute-start.6
  80.2 2.8 collective-permute-done.9
  83.1 7.9 %collective-permute-done.11 = f32[416,128]{1,0:T(8,128)S(1)} collective-permute-done((f32[416,128]{1,0:T(8,128)S(1)}, f32[416,128]{1,0:T(8,128)S(1)}, u32[]{:S(2)}, u32[]{:S(2)}) %collective-permute-start.11) | collective-permute-done | bytes 213024 | tf_op jit(solution)/shard_map/ppermute | solution.py:17
  92.0 10.2 %all_gather.13 = f32[1024,128]{1,0:T(8,128)S(1)} all-gather(f32[256,128]{1,0:T(8,128)S(1)} %fusion.54), channel_id=1, replica_groups=mesh['series'=4,'tm'=8] {'series'}, dimensions={0}, use_global_device_ids=true | all-gather | bytes 655360 | tf_op jit(solution)/shard_map/all_gather | solution.py:70
  102.2 5.9 %fusion.7 = f32[2048,128]{1,0:T(8,128)S(1)} fusion(bf16[2048,1024]{1,0:T(8,128)(2,1)} %param.6, bf16[2048,1024]{1,0:T(8,128)(2,1)} %param.5, f32[1024,128]{1,0:T(8,128)S(1)} %all_gather.13, f32[2048,128]{1,0:T(8,128)S(1)} %copy-done), kind=kOutput, calls=%fused_computation.19 | convolution fusion | flops 1084751872 | bytes 11010048 | tf_op jit(solution)/shard_map/dot_general | solution.py:73
  108.2 2.6 collective-permute-done.12
  112.4 23.8 %collective-permute-done.13 = f32[2048,128]{1,0:T(8,128)S(1)} collective-permute-done((f32[2048,128]{1,0:T(8,128)S(1)}, f32[2048,128]{1,0:T(8,128)S(1)}, u32[]{:S(2)}, u32[]{:S(2)}) %collective-permute-start.13) | collective-permute-done | bytes 1048608 | tf_op jit(solution)/shard_map/ppermute | solution.py:76
  138.3 45.8 %collective-permute-done.14 = f32[2048,128]{1,0:T(8,128)S(1)} collective-permute-done((f32[2048,128]{1,0:T(8,128)S(1)}, f32[2048,128]{1,0:T(8,128)S(1)}, u32[]{:S(2)}, u32[]{:S(2)}) %collective-permute-start.14) | collective-permute-done | bytes 1048608 | tf_op jit(solution)/shard_map/ppermute | solution.py:76
  184.4 8.2 %fusion.9 = f32[1024,128]{1,0:T(8,128)} fusion(bf16[2048,1024]{1,0:T(8,128)(2,1)} %param.6, bf16[2048,1024]{1,0:T(8,128)(2,1)} %param.5, f32[1024,128]{1,0:T(8,128)S(1)} %all_gather.13, f32[2048,128]{1,0:T(8,128)S(1)} %multiply_subtract_fusion.1), kind=kOutput, calls=%fused_computation.21 | convolution fusion | flops 1084882944 | bytes 10485760 | tf_op jit(solution)/shard_map/dot_general | solution.py:60
  195.4 3.0 collective-permute-start.15
  205.1 3.0 collective-permute-done.18
  208.2 7.9 %collective-permute-done.20 = f32[416,128]{1,0:T(8,128)S(1)} collective-permute-done((f32[416,128]{1,0:T(8,128)S(1)}, f32[416,128]{1,0:T(8,128)S(1)}, u32[]{:S(2)}, u32[]{:S(2)}) %collective-permute-start.20) | collective-permute-done | bytes 213024 | tf_op jit(solution)/shard_map/ppermute | solution.py:17
  217.2 10.0 %all_gather.14 = f32[1024,128]{1,0:T(8,128)S(1)} all-gather(f32[256,128]{1,0:T(8,128)S(1)} %fusion.44), channel_id=1, replica_groups=mesh['series'=4,'tm'=8] {'series'}, dimensions={0}, use_global_device_ids=true | all-gather | bytes 655360 | tf_op jit(solution)/shard_map/all_gather | solution.py:70
  227.2 8.2 %fusion.8 = f32[1024,128]{1,0:T(8,128)} fusion(bf16[2048,1024]{1,0:T(8,128)(2,1)} %param.6, bf16[2048,1024]{1,0:T(8,128)(2,1)} %param.5, f32[1024,128]{1,0:T(8,128)S(1)} %all_gather.14, f32[2048,128]{1,0:T(8,128)S(1)} %multiply_subtract_fusion.1), kind=kOutput, calls=%fused_computation.20 | convolution fusion | flops 1084882944 | bytes 10485760 | tf_op jit(solution)/shard_map/dot_general | solution.py:60
  236.9 4.0 %collective-permute-start.22 = (f32[416,128]{1,0:T(8,128)S(1)}, f32[416,128]{1,0:T(8,128)S(1)}, u32[]{:S(2)}, u32[]{:S(2)}) collective-permute-start(f32[416,128]{1,0:T(8,128)S(1)} %slice.172), channel_id=1, source_target_pairs={{0,2},{1,3},{2,4},{3,5},{4,6},{5,7},{8,10},{9,11},{10,12},{11,13},... | collective-permute-start | bytes 638984 | tf_op jit(solution)/shard_map/ppermute | solution.py:17
  240.9 3.5 collective-permute-start.21
  250.9 2.6 collective-permute-done.24
  253.5 7.9 %collective-permute-done.26 = f32[416,128]{1,0:T(8,128)S(1)} collective-permute-done((f32[416,128]{1,0:T(8,128)S(1)}, f32[416,128]{1,0:T(8,128)S(1)}, u32[]{:S(2)}, u32[]{:S(2)}) %collective-permute-start.26) | collective-permute-done | bytes 213024 | tf_op jit(solution)/shard_map/ppermute | solution.py:17
  262.4 9.7 %all_gather.15 = f32[1024,128]{1,0:T(8,128)S(1)} all-gather(f32[256,128]{1,0:T(8,128)S(1)} %fusion.34), channel_id=1, replica_groups=mesh['series'=4,'tm'=8] {'series'}, dimensions={0}, use_global_device_ids=true | all-gather | bytes 655360 | tf_op jit(solution)/shard_map/all_gather | solution.py:70
  272.1 5.9 %fusion.6 = f32[2048,128]{1,0:T(8,128)S(1)} fusion(bf16[2048,1024]{1,0:T(8,128)(2,1)} %param.6, bf16[2048,1024]{1,0:T(8,128)(2,1)} %param.5, f32[1024,128]{1,0:T(8,128)S(1)} %all_gather.15, f32[2048,128]{1,0:T(8,128)S(1)} %multiply_subtract_fusion.1), kind=kOutput, calls=%fused_computation.18 | convolution fusion | flops 1084751872 | bytes 11010048 | tf_op jit(solution)/shard_map/dot_general | solution.py:73
  278.1 2.6 collective-permute-done.27
  282.4 23.7 %collective-permute-done.28 = f32[2048,128]{1,0:T(8,128)S(1)} collective-permute-done((f32[2048,128]{1,0:T(8,128)S(1)}, f32[2048,128]{1,0:T(8,128)S(1)}, u32[]{:S(2)}, u32[]{:S(2)}) %collective-permute-start.28) | collective-permute-done | bytes 1048608 | tf_op jit(solution)/shard_map/ppermute | solution.py:76
  306.2 2.8 collective-permute-start.29
  309.0 45.1 %collective-permute-done.29 = f32[2048,128]{1,0:T(8,128)S(1)} collective-permute-done((f32[2048,128]{1,0:T(8,128)S(1)}, f32[2048,128]{1,0:T(8,128)S(1)}, u32[]{:S(2)}, u32[]{:S(2)}) %collective-permute-start.29) | collective-permute-done | bytes 1048608 | tf_op jit(solution)/shard_map/ppermute | solution.py:76
  (100 shorter events, 47.5 us)
Async XLA Ops:
  7.2 38.4 %reduce-scatter.5.cloned.1.call-start = ((), (), s32[]{:S(2)}) async-start(), calls=%async_computation.4 | async-start | bytes 655360 | tf_op jit(solution)/shard_map/reduce_scatter | solution.py:64
  16.2 74.7 %reduce-scatter.7.cloned.1.call-start = ((), (), s32[]{:S(2)}) async-start(), calls=%async_computation.5 | async-start | bytes 655360 | tf_op jit(solution)/shard_map/reduce_scatter | solution.py:64
  16.3 15.3 %collective-permute-start.2 = (f32[608,128]{1,0:T(8,128)S(1)}, f32[608,128]{1,0:T(8,128)S(1)}, u32[]{:S(2)}, u32[]{:S(2)}) collective-permute-start(f32[608,128]{1,0:T(8,128)S(1)} %slice.121), channel_id=1, source_target_pairs={{0,1},{1,2},{2,3},{3,4},{4,5},{5,6},{6,7},{8,9},{9,10},{10,11},{11... | collective-permute-start | bytes 933896 | tf_op jit(solution)/shard_map/ppermute | solution.py:17
  18.9 8.1 %collective-permute-start = (f32[1,128]{1,0:T(1,128)S(1)}, f32[1,128]{1,0:T(1,128)S(1)}, u32[]{:S(2)}, u32[]{:S(2)}) collective-permute-start(f32[1,128]{1,0:T(1,128)S(1)} %slice.117), channel_id=1, source_target_pairs={{0,1},{1,2},{2,3},{3,4},{4,5},{5,6},{6,7},{8,9},{9,10},{10,11},{11... | collective-permute-start | bytes 1544 | tf_op jit(solution)/shard_map/ppermute | solution.py:17
  23.5 8.2 %collective-permute-start.1 = (f32[416,128]{1,0:T(8,128)S(1)}, f32[416,128]{1,0:T(8,128)S(1)}, u32[]{:S(2)}, u32[]{:S(2)}) collective-permute-start(f32[416,128]{1,0:T(8,128)S(1)} %slice.120), channel_id=1, source_target_pairs={{0,2},{1,3},{2,4},{3,5},{4,6},{5,7},{8,10},{9,11},{10,12},{11,13},... | collective-permute-start | bytes 638984 | tf_op jit(solution)/shard_map/ppermute | solution.py:17
  31.8 13.8 %collective-permute-start.4 = (f32[608,128]{1,0:T(8,128)S(1)}, f32[608,128]{1,0:T(8,128)S(1)}, u32[]{:S(2)}, u32[]{:S(2)}) collective-permute-start(f32[608,128]{1,0:T(8,128)S(1)} %slice.152), channel_id=1, source_target_pairs={{1,0},{2,1},{3,2},{4,3},{5,4},{6,5},{7,6},{9,8},{10,9},{11,10},{12... | collective-permute-start | bytes 933896 | tf_op jit(solution)/shard_map/ppermute | solution.py:17
  33.8 11.8 %collective-permute-start.5 = (f32[416,128]{1,0:T(8,128)}, f32[416,128]{1,0:T(8,128)S(1)}, u32[]{:S(2)}, u32[]{:S(2)}) collective-permute-start(f32[416,128]{1,0:T(8,128)} %slice.153), channel_id=1, source_target_pairs={{2,0},{3,1},{4,2},{5,3},{6,4},{7,5},{10,8},{11,9},{12,10},{13,11},... | collective-permute-start | bytes 638984 | tf_op jit(solution)/shard_map/ppermute | solution.py:17
  35.1 3.7 %collective-permute-start.3 = (f32[1,128]{1,0:T(1,128)S(1)}, f32[1,128]{1,0:T(1,128)S(1)}, u32[]{:S(2)}, u32[]{:S(2)}) collective-permute-start(f32[1,128]{1,0:T(1,128)S(1)} %slice.151), channel_id=1, source_target_pairs={{1,0},{2,1},{3,2},{4,3},{5,4},{6,5},{7,6},{9,8},{10,9},{11,10},{12... | collective-permute-start | bytes 1544 | tf_op jit(solution)/shard_map/ppermute | solution.py:17
  65.0 151.2 %reduce-scatter.9.cloned.1.call-start = ((), (), s32[]{:S(2)}) async-start(), calls=%async_computation.6 | async-start | bytes 655360 | tf_op jit(solution)/shard_map/reduce_scatter | solution.py:64
  65.1 11.1 %collective-permute-start.8 = (f32[608,128]{1,0:T(8,128)S(1)}, f32[608,128]{1,0:T(8,128)S(1)}, u32[]{:S(2)}, u32[]{:S(2)}) collective-permute-start(f32[608,128]{1,0:T(8,128)S(1)} %slice.157), channel_id=1, source_target_pairs={{0,1},{1,2},{2,3},{3,4},{4,5},{5,6},{6,7},{8,9},{9,10},{10,11},{11... | collective-permute-start | bytes 933896 | tf_op jit(solution)/shard_map/ppermute | solution.py:17
  66.4 9.7 %collective-permute-start.7 = (f32[416,128]{1,0:T(8,128)S(1)}, f32[416,128]{1,0:T(8,128)S(1)}, u32[]{:S(2)}, u32[]{:S(2)}) collective-permute-start(f32[416,128]{1,0:T(8,128)S(1)} %slice.156), channel_id=1, source_target_pairs={{0,2},{1,3},{2,4},{3,5},{4,6},{5,7},{8,10},{9,11},{10,12},{11,13},... | collective-permute-start | bytes 638984 | tf_op jit(solution)/shard_map/ppermute | solution.py:17
  70.5 3.6 collective-permute-start.6
  76.3 14.6 %collective-permute-start.10 = (f32[608,128]{1,0:T(8,128)S(1)}, f32[608,128]{1,0:T(8,128)S(1)}, u32[]{:S(2)}, u32[]{:S(2)}) collective-permute-start(f32[608,128]{1,0:T(8,128)S(1)} %slice.160), channel_id=1, source_target_pairs={{1,0},{2,1},{3,2},{4,3},{5,4},{6,5},{7,6},{9,8},{10,9},{11,10},{12... | collective-permute-start | bytes 933896 | tf_op jit(solution)/shard_map/ppermute | solution.py:17
  77.6 13.3 %collective-permute-start.11 = (f32[416,128]{1,0:T(8,128)S(1)}, f32[416,128]{1,0:T(8,128)S(1)}, u32[]{:S(2)}, u32[]{:S(2)}) collective-permute-start(f32[416,128]{1,0:T(8,128)S(1)} %slice.161), channel_id=1, source_target_pairs={{2,0},{3,1},{4,2},{5,3},{6,4},{7,5},{10,8},{11,9},{12,10},{13,11},... | collective-permute-start | bytes 638984 | tf_op jit(solution)/shard_map/ppermute | solution.py:17
  78.9 4.2 %collective-permute-start.9 = (f32[1,128]{1,0:T(1,128)S(1)}, f32[1,128]{1,0:T(1,128)S(1)}, u32[]{:S(2)}, u32[]{:S(2)}) collective-permute-start(f32[1,128]{1,0:T(1,128)S(1)} %slice.159), channel_id=1, source_target_pairs={{1,0},{2,1},{3,2},{4,3},{5,4},{6,5},{7,6},{9,8},{10,9},{11,10},{12... | collective-permute-start | bytes 1544 | tf_op jit(solution)/shard_map/ppermute | solution.py:17
  110.9 25.3 %collective-permute-start.13 = (f32[2048,128]{1,0:T(8,128)S(1)}, f32[2048,128]{1,0:T(8,128)S(1)}, u32[]{:S(2)}, u32[]{:S(2)}) collective-permute-start(f32[2048,128]{1,0:T(8,128)S(1)} %add.57), channel_id=1, source_target_pairs={{0,2},{1,3},{2,0},{3,1},{4,6},{5,7},{6,4},{7,5},{8,10},{9,11},{10,... | collective-permute-start | bytes 3145736 | tf_op jit(solution)/shard_map/ppermute | solution.py:76
  136.3 47.8 %collective-permute-start.14 = (f32[2048,128]{1,0:T(8,128)S(1)}, f32[2048,128]{1,0:T(8,128)S(1)}, u32[]{:S(2)}, u32[]{:S(2)}) collective-permute-start(f32[2048,128]{1,0:T(8,128)S(1)} %add.58), channel_id=1, source_target_pairs={{0,4},{1,5},{2,6},{3,7},{4,0},{5,1},{6,2},{7,3},{8,12},{9,13},{10,... | collective-permute-start | bytes 3145736 | tf_op jit(solution)/shard_map/ppermute | solution.py:76
  192.6 68.7 %reduce-scatter.11.cloned.1.call-start = ((), (), s32[]{:S(2)}) async-start(), calls=%async_computation.7 | async-start | bytes 655360 | tf_op jit(solution)/shard_map/reduce_scatter | solution.py:64
  192.7 8.3 %collective-permute-start.17 = (f32[608,128]{1,0:T(8,128)S(1)}, f32[608,128]{1,0:T(8,128)S(1)}, u32[]{:S(2)}, u32[]{:S(2)}) collective-permute-start(f32[608,128]{1,0:T(8,128)S(1)} %slice.165), channel_id=1, source_target_pairs={{0,1},{1,2},{2,3},{3,4},{4,5},{5,6},{6,7},{8,9},{9,10},{10,11},{11... | collective-permute-start | bytes 933896 | tf_op jit(solution)/shard_map/ppermute | solution.py:17
  194.0 7.0 %collective-permute-start.16 = (f32[416,128]{1,0:T(8,128)S(1)}, f32[416,128]{1,0:T(8,128)S(1)}, u32[]{:S(2)}, u32[]{:S(2)}) collective-permute-start(f32[416,128]{1,0:T(8,128)S(1)} %slice.164), channel_id=1, source_target_pairs={{0,2},{1,3},{2,4},{3,5},{4,6},{5,7},{8,10},{9,11},{10,12},{11,13},... | collective-permute-start | bytes 638984 | tf_op jit(solution)/shard_map/ppermute | solution.py:17
  195.4 3.8 %collective-permute-start.15 = (f32[1,128]{1,0:T(1,128)S(1)}, f32[1,128]{1,0:T(1,128)S(1)}, u32[]{:S(2)}, u32[]{:S(2)}) collective-permute-start(f32[1,128]{1,0:T(1,128)S(1)} %slice.162), channel_id=1, source_target_pairs={{0,1},{1,2},{2,3},{3,4},{4,5},{5,6},{6,7},{8,9},{9,10},{10,11},{11... | collective-permute-start | bytes 1544 | tf_op jit(solution)/shard_map/ppermute | solution.py:17
  201.2 14.9 %collective-permute-start.19 = (f32[608,128]{1,0:T(8,128)S(1)}, f32[608,128]{1,0:T(8,128)S(1)}, u32[]{:S(2)}, u32[]{:S(2)}) collective-permute-start(f32[608,128]{1,0:T(8,128)S(1)} %slice.168), channel_id=1, source_target_pairs={{1,0},{2,1},{3,2},{4,3},{5,4},{6,5},{7,6},{9,8},{10,9},{11,10},{12... | collective-permute-start | bytes 933896 | tf_op jit(solution)/shard_map/ppermute | solution.py:17
  202.5 13.5 %collective-permute-start.20 = (f32[416,128]{1,0:T(8,128)S(1)}, f32[416,128]{1,0:T(8,128)S(1)}, u32[]{:S(2)}, u32[]{:S(2)}) collective-permute-start(f32[416,128]{1,0:T(8,128)S(1)} %slice.169), channel_id=1, source_target_pairs={{2,0},{3,1},{4,2},{5,3},{6,4},{7,5},{10,8},{11,9},{12,10},{13,11},... | collective-permute-start | bytes 638984 | tf_op jit(solution)/shard_map/ppermute | solution.py:17
  203.8 4.4 %collective-permute-start.18 = (f32[1,128]{1,0:T(1,128)S(1)}, f32[1,128]{1,0:T(1,128)S(1)}, u32[]{:S(2)}, u32[]{:S(2)}) collective-permute-start(f32[1,128]{1,0:T(1,128)S(1)} %slice.167), channel_id=1, source_target_pairs={{1,0},{2,1},{3,2},{4,3},{5,4},{6,5},{7,6},{9,8},{10,9},{11,10},{12... | collective-permute-start | bytes 1544 | tf_op jit(solution)/shard_map/ppermute | solution.py:17
  235.5 11.0 %collective-permute-start.23 = (f32[608,128]{1,0:T(8,128)S(1)}, f32[608,128]{1,0:T(8,128)S(1)}, u32[]{:S(2)}, u32[]{:S(2)}) collective-permute-start(f32[608,128]{1,0:T(8,128)S(1)} %slice.173), channel_id=1, source_target_pairs={{0,1},{1,2},{2,3},{3,4},{4,5},{5,6},{6,7},{8,9},{9,10},{10,11},{11... | collective-permute-start | bytes 933896 | tf_op jit(solution)/shard_map/ppermute | solution.py:17
  236.9 9.6 %collective-permute-start.22 = (f32[416,128]{1,0:T(8,128)S(1)}, f32[416,128]{1,0:T(8,128)S(1)}, u32[]{:S(2)}, u32[]{:S(2)}) collective-permute-start(f32[416,128]{1,0:T(8,128)S(1)} %slice.172), channel_id=1, source_target_pairs={{0,2},{1,3},{2,4},{3,5},{4,6},{5,7},{8,10},{9,11},{10,12},{11,13},... | collective-permute-start | bytes 638984 | tf_op jit(solution)/shard_map/ppermute | solution.py:17
  240.9 4.3 %collective-permute-start.21 = (f32[1,128]{1,0:T(1,128)S(1)}, f32[1,128]{1,0:T(1,128)S(1)}, u32[]{:S(2)}, u32[]{:S(2)}) collective-permute-start(f32[1,128]{1,0:T(1,128)S(1)} %slice.170), channel_id=1, source_target_pairs={{0,1},{1,2},{2,3},{3,4},{4,5},{5,6},{6,7},{8,9},{9,10},{10,11},{11... | collective-permute-start | bytes 1544 | tf_op jit(solution)/shard_map/ppermute | solution.py:17
  246.7 14.6 %collective-permute-start.25 = (f32[608,128]{1,0:T(8,128)S(1)}, f32[608,128]{1,0:T(8,128)S(1)}, u32[]{:S(2)}, u32[]{:S(2)}) collective-permute-start(f32[608,128]{1,0:T(8,128)S(1)} %slice.176), channel_id=1, source_target_pairs={{1,0},{2,1},{3,2},{4,3},{5,4},{6,5},{7,6},{9,8},{10,9},{11,10},{12... | collective-permute-start | bytes 933896 | tf_op jit(solution)/shard_map/ppermute | solution.py:17
  248.0 13.3 %collective-permute-start.26 = (f32[416,128]{1,0:T(8,128)S(1)}, f32[416,128]{1,0:T(8,128)S(1)}, u32[]{:S(2)}, u32[]{:S(2)}) collective-permute-start(f32[416,128]{1,0:T(8,128)S(1)} %slice.177), channel_id=1, source_target_pairs={{2,0},{3,1},{4,2},{5,3},{6,4},{7,5},{10,8},{11,9},{12,10},{13,11},... | collective-permute-start | bytes 638984 | tf_op jit(solution)/shard_map/ppermute | solution.py:17
  249.3 4.2 %collective-permute-start.24 = (f32[1,128]{1,0:T(1,128)S(1)}, f32[1,128]{1,0:T(1,128)S(1)}, u32[]{:S(2)}, u32[]{:S(2)}) collective-permute-start(f32[1,128]{1,0:T(1,128)S(1)} %slice.175), channel_id=1, source_target_pairs={{1,0},{2,1},{3,2},{4,3},{5,4},{6,5},{7,6},{9,8},{10,9},{11,10},{12... | collective-permute-start | bytes 1544 | tf_op jit(solution)/shard_map/ppermute | solution.py:17
  280.8 25.3 %collective-permute-start.28 = (f32[2048,128]{1,0:T(8,128)S(1)}, f32[2048,128]{1,0:T(8,128)S(1)}, u32[]{:S(2)}, u32[]{:S(2)}) collective-permute-start(f32[2048,128]{1,0:T(8,128)S(1)} %add.63), channel_id=1, source_target_pairs={{0,2},{1,3},{2,0},{3,1},{4,6},{5,7},{6,4},{7,5},{8,10},{9,11},{10,... | collective-permute-start | bytes 3145736 | tf_op jit(solution)/shard_map/ppermute | solution.py:76
  306.2 47.9 %collective-permute-start.29 = (f32[2048,128]{1,0:T(8,128)S(1)}, f32[2048,128]{1,0:T(8,128)S(1)}, u32[]{:S(2)}, u32[]{:S(2)}) collective-permute-start(f32[2048,128]{1,0:T(8,128)S(1)} %add.64), channel_id=1, source_target_pairs={{0,4},{1,5},{2,6},{3,7},{4,0},{5,1},{6,2},{7,3},{8,12},{9,13},{10,... | collective-permute-start | bytes 3145736 | tf_op jit(solution)/shard_map/ppermute | solution.py:76
  (5 other events, 74.9 us)
Sparse Core Ops, SparseCore 0:
  16.3 27.8 reduce-scatter.4
  65.1 23.8 reduce-scatter.6
  192.7 23.4 reduce-scatter.8
  235.6 25.3 reduce-scatter.10
